TPU v7x, 256 devices: a whole 4x4x8 slice. The times are simulated.
256 devices in a mesh: dp: 32 (over z, y), ep: 8 (over x, core).
Axes of the slice: x: 4, y: 4, z: 8, core: 2. Of those that a mesh axis runs over, the one named last changes fastest.
Arguments:
- states: bfloat16 [2048, 16, 128, 128], P(('dp', 'ep')), may hold values from -4 to 4
- query_rows: bfloat16 [2048, 4, 1024], P(('dp', 'ep')), may hold values from -6 to 6
- key_rows: bfloat16 [2048, 4, 1024], P(('dp', 'ep')), may hold values from -6 to 6
- value_rows: bfloat16 [2048, 4, 2048], P(('dp', 'ep')), may hold values from -6 to 6
- gate_rows: bfloat16 [2048, 4, 2048], P(('dp', 'ep')), may hold values from -6 to 6
- beta_logit: bfloat16 [2048, 4, 16], P(('dp', 'ep')), may hold values from -6 to 6
- decay_logit: bfloat16 [2048, 4, 16], P(('dp', 'ep')), may hold values from -8 to 8
- residual: bfloat16 [2048, 4, 2048], P(('dp', 'ep')), may hold values from -6 to 6
- route_ids: int32 [2048, 4, 10], P(('dp', 'ep')), may hold values from 0 to 255, all different within a row; in each aligned block of 32 rows (0 to 31, 32 to 63, ..., all dimensions but the last counted through in order) at most 3 rows name the same one
- route_prob: float32 [2048, 4, 10], P(('dp', 'ep')), may hold values from 0.05 to 1
- out_weight: bfloat16 [2048, 2048], P(None, 'ep'), may hold values from -0.125 to 0.125
- core_gain: float32 [128], replicated, may hold values from 0.1 to 1.9
- moe_gain: float32 [2048], replicated, may hold values from 0.1 to 1.9
- gate_up: bfloat16 [256, 2048, 512], P(('dp', 'ep')), may hold values from -0.125 to 0.125
- down_weight: bfloat16 [256, 256, 2048], P(('dp', 'ep')), may hold values from -0.375 to 0.375
- new_home: int32 [2048], P(('dp', 'ep')), may hold values from 0 to 2047, as said below
Outputs:
- mixed_out: bfloat16 [2048, 4, 2048], P(('dp', 'ep'))
- moved_out: bfloat16 [2048, 16, 128, 128], P(('dp', 'ep'))
Inputs may be any that keep to these rules, and one draw needn't show every extreme that they name: `route_ids`: each row names 10 different experts; among the 32 rows of one device (its requests, each with its 4 tokens) no expert is named more than 3 times, a bound that some block reaches. `new_home`: A permutation of the request positions; a request stays among the 8 devices of its dp index, and every device hands exactly 1 of its requests to each device of that group, itself included.
All inputs are finite; a program needn't handle non-finite values.
Results may differ from a plain program's by a relative error of at most 0.01.
Values may be sent and summed in bfloat16 or wider, within the bound.
A program may use at most 128 MiB of HBM per device.

v0:
```python
import jax
import jax.numpy as jnp
from jax import lax
from jax.sharding import PartitionSpec as P

epsilon = 1e-06


def unit_rows(values):
    return values * lax.rsqrt(jnp.sum(values * values, -1, keepdims=True) + epsilon)


def delta_block(
    state_in, query_rows, key_rows, value_rows, gate_rows, beta_logit, decay_logit, core_gain
):
    batch_size = state_in.shape[0]
    head_count = decay_logit.shape[-1]
    head_width = state_in.shape[-1]
    key_heads = query_rows.shape[-1] // head_width
    repeats = head_count // key_heads
    memory_state = state_in.astype(jnp.float32)
    outputs = []
    for position in range(query_rows.shape[1]):
        queries = unit_rows(
            query_rows[:, position].astype(jnp.float32).reshape(batch_size, key_heads, head_width)
        )
        queries = jnp.repeat(queries, repeats, axis=1) * head_width ** (-0.5)
        key_units = unit_rows(
            key_rows[:, position].astype(jnp.float32).reshape(batch_size, key_heads, head_width)
        )
        key_units = jnp.repeat(key_units, repeats, axis=1)
        values = (
            value_rows[:, position].astype(jnp.float32).reshape(batch_size, head_count, head_width)
        )
        decays = jax.nn.sigmoid(decay_logit[:, position].astype(jnp.float32))
        strength = jax.nn.sigmoid(beta_logit[:, position].astype(jnp.float32))
        memory_state = memory_state * decays[:, :, None, None]
        memory = jnp.einsum(
            "bhkv,bhk->bhv", memory_state, key_units, precision=lax.Precision.HIGHEST
        )
        update = (values - memory) * strength[:, :, None]
        memory_state = memory_state + key_units[:, :, :, None] * update[:, :, None, :]
        reading = jnp.einsum(
            "bhkv,bhk->bhv", memory_state, queries, precision=lax.Precision.HIGHEST
        )
        scaled = reading * lax.rsqrt(jnp.mean(reading * reading, -1, keepdims=True) + epsilon)
        gate_vals = (
            gate_rows[:, position].astype(jnp.float32).reshape(batch_size, head_count, head_width)
        )
        gated_out = scaled * core_gain * jax.nn.silu(gate_vals)
        outputs.append(gated_out.reshape(batch_size, head_count * head_width).astype(jnp.bfloat16))
    return (memory_state.astype(jnp.bfloat16), jnp.stack(outputs, axis=1))


def rms_scale(values, gain):
    return values * lax.rsqrt(jnp.mean(values * values, -1, keepdims=True) + epsilon) * gain


def expert_apply(chosen_rows, gate_up, down_weight):
    hidden_units = down_weight.shape[0]
    joined = jnp.dot(chosen_rows, gate_up, preferred_element_type=jnp.float32)
    active = (jax.nn.silu(joined[:, :hidden_units]) * joined[:, hidden_units:]).astype(jnp.bfloat16)
    return jnp.dot(active, down_weight, preferred_element_type=jnp.float32).astype(jnp.bfloat16)


def pack(values, positions, lane_count):
    zeroed = jnp.zeros(values.shape, values.dtype)
    placed = zeroed.at[positions].set(values)
    return placed.reshape((lane_count, values.shape[0] // lane_count) + values.shape[1:])


def unpack(values):
    return values.reshape((values.shape[0] * values.shape[1],) + values.shape[2:])


def shards(
    states,
    query_rows,
    key_rows,
    value_rows,
    gate_rows,
    beta_logit,
    decay_logit,
    residual,
    route_ids,
    route_prob,
    out_weight,
    core_gain,
    moe_gain,
    gate_up,
    down_weight,
    new_home,
):
    req_count = states.shape[0]
    step_count = query_rows.shape[1]
    model_width = residual.shape[-1]
    ep_size = lax.axis_size("ep")
    dp_size = lax.axis_size("dp")
    target = new_home // req_count % ep_size
    new_place = new_home % req_count
    order_ids = jnp.arange(req_count, dtype=jnp.int32)
    earlier = (target[:, None] == target[None, :]) & (order_ids[None, :] < order_ids[:, None])
    lane_rank = jnp.sum(earlier.astype(jnp.int32), axis=1)
    lane_cap = req_count // ep_size
    buffer_index = target * lane_cap + lane_rank
    fresh_states, core_out = delta_block(
        states, query_rows, key_rows, value_rows, gate_rows, beta_logit, decay_logit, core_gain
    )
    received = (
        lax.all_to_all(
            pack(fresh_states, buffer_index, ep_size), "ep", split_axis=0, concat_axis=0, tiled=True
        ),
        lax.all_to_all(
            pack(new_place, buffer_index, ep_size), "ep", split_axis=0, concat_axis=0, tiled=True
        ),
    )
    moved_out = jnp.zeros_like(states).at[unpack(received[1])].set(unpack(received[0]), mode="drop")
    token_count = req_count * step_count
    core_flat = core_out.reshape(token_count, core_out.shape[-1])
    columns = jnp.dot(
        lax.all_gather(core_flat, "ep", axis=0, tiled=True),
        out_weight,
        preferred_element_type=jnp.float32,
    ).astype(jnp.bfloat16)
    attention = lax.all_to_all(columns, "ep", split_axis=0, concat_axis=1, tiled=True)
    hidden = (
        residual.reshape(token_count, model_width).astype(jnp.float32)
        + attention.astype(jnp.float32)
    ).astype(jnp.bfloat16)
    normed = rms_scale(hidden.astype(jnp.float32), moe_gain).astype(jnp.bfloat16)
    top_count = route_ids.shape[-1]
    experts = dp_size * ep_size
    capacity = (token_count * top_count + experts - 1) // experts + 1
    flat_ids = route_ids.reshape(-1)
    onehot = (flat_ids[:, None] == jnp.arange(experts, dtype=jnp.int32)[None, :]).astype(jnp.int32)
    route_rank = jnp.sum(jnp.cumsum(onehot, axis=0) * onehot, axis=1) - 1
    slot_index = flat_ids * capacity + route_rank
    outgoing = (
        jnp.zeros((experts * capacity, model_width), jnp.bfloat16)
        .at[slot_index]
        .set(jnp.repeat(normed, top_count, axis=0))
    )
    arrived = lax.all_to_all(
        lax.all_to_all(
            outgoing.reshape(dp_size, ep_size, capacity, model_width),
            "dp",
            split_axis=0,
            concat_axis=0,
            tiled=True,
        ),
        "ep",
        split_axis=1,
        concat_axis=1,
        tiled=True,
    )
    result = expert_apply(arrived.reshape(-1, model_width), gate_up[0], down_weight[0]).reshape(
        dp_size, ep_size, capacity, model_width
    )
    returned = lax.all_to_all(
        lax.all_to_all(result, "dp", split_axis=0, concat_axis=0, tiled=True),
        "ep",
        split_axis=1,
        concat_axis=1,
        tiled=True,
    )
    routed = returned.reshape(experts * capacity, model_width)[slot_index]
    weights = route_prob.reshape(token_count, top_count)
    weights = weights / jnp.sum(weights, -1, keepdims=True)
    combined = jnp.sum(
        routed.reshape(token_count, top_count, model_width).astype(jnp.float32)
        * weights[:, :, None],
        axis=1,
    )
    mixed_out = (
        (hidden.astype(jnp.float32) + combined)
        .astype(jnp.bfloat16)
        .reshape(req_count, step_count, model_width)
    )
    return (mixed_out, moved_out)


def solution(mesh):
    placed = (
        P(("dp", "ep"), None, None, None),
        P(("dp", "ep"), None, None),
        P(("dp", "ep"), None, None),
        P(("dp", "ep"), None, None),
        P(("dp", "ep"), None, None),
        P(("dp", "ep"), None, None),
        P(("dp", "ep"), None, None),
        P(("dp", "ep"), None, None),
        P(("dp", "ep"), None, None),
        P(("dp", "ep"), None, None),
        P(None, "ep"),
        P(),
        P(),
        P(("dp", "ep"), None, None),
        P(("dp", "ep"), None, None),
        P(("dp", "ep")),
    )
    return jax.shard_map(
        shards,
        mesh=mesh,
        in_specs=placed,
        out_specs=(P(("dp", "ep"), None, None), P(("dp", "ep"), None, None, None)),
        check_vma=False,
    )
```

profile of v0, /device:TPU:24, one launch (start us, length us, event | category | flops | bytes accessed | tf_op | source)
XLA Modules:
  0.0 571.1 jit_solution(461292190551067246)
XLA Ops:
  14.3 9.7 %fusion = f32[8,16,1,128]{3,2,1,0:T(1,128)S(1)} fusion(f32[8,16,128,1]{2,3,1,0:T(1,128)S(1)} %bitcast.152, bf16[8,16,128,128]{3,2,1,0:T(8,128)(2,1)} %param.16, f32[8,16]{1,0:T(8,128)S(1)} %get-tuple-element.37), kind=kOutput, calls=%fused_computation.10 | convolution fusion | flops 29360128 | bytes 4325888 | tf_op jit(solution)/shard_map/bhkv,bhk->bhv/dot_general | solution.py:38
  24.1 8.3 %fusion.2 = f32[8,16,1,128]{3,2,1,0:T(1,128)S(1)} fusion(f32[8,16,128,1]{2,3,1,0:T(1,128)S(1)} %bitcast.196, bf16[8,16,128,128]{3,2,1,0:T(8,128)(2,1)S(1)} %copy-done.1, f32[8,16,128]{2,1,0:T(8,128)S(1)} %subtract_multiply_fusion.3, f32[8,16,128]{2,1,0:T(8,128)S(1)} %bitcast.153, f32[8,16]{1,0:T(8,128)S(1)} %get-tuple-element.37), kind=kOutput, calls=%fused_computation.12 | convolution fusion | flops 33554432 | bytes 4456960 | tf_op jit(solution)/shard_map/bhkv,bhk->bhv/dot_general | solution.py:43
  32.6 9.0 %fusion.3 = f32[8,16,1,128]{3,2,1,0:T(1,128)S(1)} fusion(f32[8,16,128,1]{2,3,1,0:T(1,128)S(1)} %bitcast.161, bf16[8,16,128,128]{3,2,1,0:T(8,128)(2,1)S(1)} %copy-done.1, f32[8,16]{1,0:T(8,128)S(1)} %get-tuple-element.36, f32[8,16,128]{2,1,0:T(8,128)S(1)} %subtract_multiply_fusion.3, f32[8,16,128]{2,1,0:T(8,128)S(1)} %bitcast.154, ...), kind=kOutput, calls=%fused_computation.13 | convolution fusion | flops 35651584 | bytes 4457472 | tf_op jit(solution)/shard_map/bhkv,bhk->bhv/dot_general | solution.py:38
  41.7 11.6 %fusion.11 = f32[8,16,1,128]{3,2,1,0:T(1,128)S(1)} fusion(f32[8,16,128,1]{2,3,1,0:T(1,128)S(1)} %bitcast.197, bf16[8,16,128,128]{3,2,1,0:T(8,128)(2,1)S(1)} %copy-done.1, f32[8,16,128]{2,1,0:T(8,128)S(1)} %subtract_multiply_fusion.2, f32[8,16,128]{2,1,0:T(8,128)S(1)} %bitcast.162, f32[8,16]{1,0:T(8,128)S(1)} %get-tuple-element.36, ...), kind=kOutput, calls=%fused_computation.20 | convolution fusion | flops 39845888 | bytes 4588544 | tf_op jit(solution)/shard_map/bhkv,bhk->bhv/dot_general | solution.py:43
  53.4 11.7 %fusion.7 = f32[8,16,1,128]{3,2,1,0:T(1,128)S(1)} fusion(f32[8,16,128,1]{2,3,1,0:T(1,128)S(1)} %bitcast.168, bf16[8,16,128,128]{3,2,1,0:T(8,128)(2,1)S(1)} %copy-done.1, f32[8,16]{1,0:T(8,128)S(1)} %get-tuple-element.35, f32[8,16,128]{2,1,0:T(8,128)S(1)} %subtract_multiply_fusion.2, f32[8,16,128]{2,1,0:T(8,128)S(1)} %bitcast.163, ...), kind=kOutput, calls=%fused_computation.16 | convolution fusion | flops 41943040 | bytes 4589056 | tf_op jit(solution)/shard_map/bhkv,bhk->bhv/dot_general | solution.py:38
  65.2 15.5 %fusion.43 = f32[8,16,1,128]{3,2,1,0:T(1,128)S(1)} fusion(f32[8,16,128,1]{2,3,1,0:T(1,128)S(1)} %bitcast.198, bf16[8,16,128,128]{3,2,1,0:T(8,128)(2,1)S(1)} %copy-done.1, f32[8,16,128]{2,1,0:T(8,128)S(1)} %subtract_multiply_fusion.1, f32[8,16,128]{2,1,0:T(8,128)S(1)} %bitcast.169, f32[8,16]{1,0:T(8,128)S(1)} %get-tuple-element.35, ...), kind=kOutput, calls=%fused_computation.56 | convolution fusion | flops 46137344 | bytes 4720128 | tf_op jit(solution)/shard_map/bhkv,bhk->bhv/dot_general | solution.py:43
  80.9 15.6 %fusion.5 = f32[8,16,1,128]{3,2,1,0:T(1,128)S(1)} fusion(f32[8,16,128,1]{2,3,1,0:T(1,128)S(1)} %bitcast.173, f32[8,16]{1,0:T(8,128)S(1)} %get-tuple-element.34, bf16[8,16,128,128]{3,2,1,0:T(8,128)(2,1)S(1)} %copy-done.1, f32[8,16,128]{2,1,0:T(8,128)S(1)} %subtract_multiply_fusion.1, f32[8,16,128]{2,1,0:T(8,128)S(1)} %bitcast.170, ...), kind=kOutput, calls=%fused_computation.14 | convolution fusion | flops 48234496 | bytes 4720640 | tf_op jit(solution)/shard_map/bhkv,bhk->bhv/dot_general | solution.py:38
  96.8 21.1 %fusion.10 = f32[8,16,1,128]{3,2,1,0:T(1,128)S(1)} fusion(f32[8,16,128,1]{2,3,1,0:T(1,128)S(1)} %bitcast.199, f32[8,16,128]{2,1,0:T(8,128)S(1)} %subtract_multiply_fusion, f32[8,16,128]{2,1,0:T(8,128)S(1)} %bitcast.174, f32[8,16]{1,0:T(8,128)S(1)} %get-tuple-element.34, bf16[8,16,128,128]{3,2,1,0:T(8,128)(2,1)S(1)} %copy-done.1, ...), kind=kOutput, calls=%fused_computation.19 | convolution fusion | flops 52428800 | bytes 4851712 | tf_op jit(solution)/shard_map/bhkv,bhk->bhv/dot_general | solution.py:43
  120.4 27.7 %all-gather.2.cloned.1.call-done = bf16[256,2048]{1,0:T(8,128)(2,1)} async-done(((bf16[32,2048]{1,0:T(8,128)(2,1)}), bf16[256,2048]{1,0:T(8,128)(2,1)}) %all-gather.2.cloned.1.call-update) | async-done | bytes 1048592 | tf_op jit(solution)/shard_map/all_gather | solution.py:121
  155.1 5.3 all-to-all-done
  166.9 5.4 scatter_custom_fusion
  172.3 9.1 %reshape.504 = bf16[32,8,3,2048]{3,2,1,0:T(4,128)(2,1)} reshape(bf16[768,2048]{1,0:T(8,128)(2,1)} %scatter_custom_fusion) | data formatting | bytes 6291456 | tf_op jit(solution)/shard_map/reshape | solution.py:145
  181.4 5.5 copy.104
  186.9 82.7 %all_to_all.50 = bf16[32,8,3,2048]{3,1,2,0:T(8,128)(2,1)S(1)} all-to-all(bf16[32,8,3,2048]{3,1,2,0:T(8,128)(2,1)S(1)} %copy.104), channel_id=1, replica_groups=mesh['dp'=32,'ep'=8] {'dp'}, dimensions={0} | all-to-all | bytes 6291456 | tf_op jit(solution)/shard_map/all_to_all | solution.py:144
  273.1 4.6 all-to-all-start.2
  279.1 36.9 %all-to-all-done.2 = bf16[32,8,3,2048]{3,0,2,1:T(8,128)(2,1)} async-done(((bf16[32,8,3,2048]{3,0,2,1:T(8,128)(2,1)}), bf16[32,8,3,2048]{3,0,2,1:T(8,128)(2,1)}, u32[]{:S(2)}, u32[]{:S(2)}) %all-to-all-start.2) | async-done | bytes 3145760 | tf_op jit(solution)/shard_map/all_to_all | solution.py:143
  319.6 6.6 %copy.106 = bf16[32,8,3,2048]{3,2,1,0:T(4,128)(2,1)} copy(bf16[32,8,3,2048]{3,0,2,1:T(8,128)(2,1)} %all-to-all-done.2) | data formatting | bytes 6291456 | tf_op jit(solution)/shard_map/all_to_all | solution.py:143
  326.2 8.8 %reshape.505 = bf16[768,2048]{1,0:T(8,128)(2,1)} reshape(bf16[32,8,3,2048]{3,2,1,0:T(4,128)(2,1)} %copy.106) | data formatting | bytes 6291456 | tf_op jit(solution)/shard_map/reshape | solution.py:156
  341.5 9.1 %reshape.506 = bf16[32,8,3,2048]{3,2,1,0:T(4,128)(2,1)} reshape(bf16[768,2048]{1,0:T(8,128)(2,1)} %convolution_convert_fusion) | data formatting | bytes 6291456 | tf_op jit(solution)/shard_map/reshape | solution.py:156
  350.6 7.2 %copy.107 = bf16[32,8,3,2048]{3,1,2,0:T(8,128)(2,1)} copy(bf16[32,8,3,2048]{3,2,1,0:T(4,128)(2,1)} %reshape.506) | data formatting | bytes 6291456 | tf_op jit(solution)/shard_map/reshape | solution.py:156
  357.9 5.8 %all-to-all-start.3 = ((bf16[32,8,3,2048]{3,1,2,0:T(8,128)(2,1)}), bf16[32,8,3,2048]{3,1,2,0:T(8,128)(2,1)}, u32[]{:S(2)}, u32[]{:S(2)}) async-start(bf16[32,8,3,2048]{3,1,2,0:T(8,128)(2,1)} %copy.107), calls=%async_computation.3 | async-start | bytes 6291456 | tf_op jit(solution)/shard_map/all_to_all | solution.py:160
  363.7 13.3 %fusion.9 = bf16[8,16,128,128]{3,2,1,0:T(8,128)(2,1)} fusion(f32[8,16,128]{2,1,0:T(8,128)S(1)} %copy-done.13, f32[8,16,128]{2,1,0:T(8,128)S(1)} %bitcast.175, f32[8,16]{1,0:T(8,128)S(1)} %get-tuple-element.34, f32[8,16,128]{2,1,0:T(8,128)S(1)} %copy-done.11, f32[8,16,128]{2,1,0:T(8,128)S(1)} %bitcast.172, f32[8,16]{1,0:T(8,128)S(1)} %get-tuple-element.35, ...), kind=kLoop, calls=%fused_computation.18 | loop fusion | flops 29360128 | bytes 8914944 | tf_op jit(solution)/shard_map/convert_element_type | solution.py:52
  380.0 10.9 %scatter_fusion = bf16[8,16,128,128]{3,2,1,0:T(8,128)(2,1)} fusion(bf16[8,16,128,128]{3,2,1,0:T(8,128)(2,1)} %broadcast.332.clone, s32[8]{0:T(128)S(1)} %compare_select_fusion.2, bf16[8,16,128,128]{3,2,1,0:T(8,128)(2,1)} %fusion.9), kind=kCustom, calls=%fused_computation.3 | custom fusion | bytes 12582944 | tf_op jit(solution)/shard_map/scatter | solution.py:68
  390.9 46.9 %all-to-all-done.3 = bf16[32,8,3,2048]{3,1,2,0:T(8,128)(2,1)} async-done(((bf16[32,8,3,2048]{3,1,2,0:T(8,128)(2,1)}), bf16[32,8,3,2048]{3,1,2,0:T(8,128)(2,1)}, u32[]{:S(2)}, u32[]{:S(2)}) %all-to-all-start.3) | async-done | bytes 3145760 | tf_op jit(solution)/shard_map/all_to_all | solution.py:160
  437.7 4.8 all-to-all-start.6
  442.5 5.3 copy.108
  447.9 44.3 %all-to-all-done.6 = bf16[8,1,16,128,128]{4,3,2,1,0:T(8,128)(2,1)} async-done(((bf16[8,1,16,128,128]{4,3,2,1,0:T(8,128)(2,1)}), bf16[8,1,16,128,128]{4,3,2,1,0:T(8,128)(2,1)}, u32[]{:S(2)}, u32[]{:S(2)}) %all-to-all-start.6) | async-done | bytes 4194336 | tf_op jit(solution)/shard_map/all_to_all | solution.py:110
  500.8 10.9 %scatter_fusion.1 = bf16[8,16,128,128]{3,2,1,0:T(8,128)(2,1)} fusion(bf16[8,16,128,128]{3,2,1,0:T(8,128)(2,1)} %broadcast.332, s32[8]{0:T(128)S(1)} %fusion.54, bf16[8,16,128,128]{3,2,1,0:T(8,128)(2,1)} %bitcast.77), kind=kCustom, calls=%fused_computation.4 | custom fusion | bytes 12582944 | tf_op jit(solution)/shard_map/scatter | solution.py:117
  511.7 23.4 %all-to-all-done.4 = bf16[32,8,3,2048]{3,0,2,1:T(8,128)(2,1)} async-done(((bf16[32,8,3,2048]{3,0,2,1:T(8,128)(2,1)}), bf16[32,8,3,2048]{3,0,2,1:T(8,128)(2,1)}, u32[]{:S(2)}, u32[]{:S(2)}) %all-to-all-start.4) | async-done | bytes 3145760 | tf_op jit(solution)/shard_map/all_to_all | solution.py:159
  535.1 6.5 %copy.109 = bf16[32,8,3,2048]{3,2,1,0:T(4,128)(2,1)} copy(bf16[32,8,3,2048]{3,0,2,1:T(8,128)(2,1)} %all-to-all-done.4) | data formatting | bytes 6291456 | tf_op jit(solution)/shard_map/all_to_all | solution.py:159
  541.6 8.8 %reshape.507 = bf16[768,2048]{1,0:T(8,128)(2,1)} reshape(bf16[32,8,3,2048]{3,2,1,0:T(4,128)(2,1)} %copy.109) | data formatting | bytes 6291456 | tf_op jit(solution)/shard_map/reshape | solution.py:166
  550.4 6.8 %gather_fusion = bf16[320,2048]{1,0:T(8,128)(2,1)S(1)} fusion(bf16[768,2048]{1,0:T(8,128)(2,1)} %reshape.507, s32[1024]{0:T(1024)} %pad_clamp_fusion), kind=kCustom, calls=%fused_computation | custom fusion | bytes 2622720 | tf_op jit(solution)/shard_map/gather | solution.py:166
  (169 shorter events, 56.7 us)
Async XLA Ops:
  7.2 327.9 %copy-start = (bf16[1,2048,512]{2,1,0:T(8,128)(2,1)S(1)}, bf16[1,2048,512]{2,1,0:T(8,128)(2,1)}, u32[]{:S(2)}) copy-start(bf16[1,2048,512]{2,1,0:T(8,128)(2,1)} %param.29) | copy-start | bytes 6291460
  7.2 140.9 %all-gather.2.cloned.1.call-start = ((), (), s32[]{:S(2)}) async-start(), calls=%async_computation.7 | async-start | bytes 1179648 | tf_op jit(solution)/shard_map/all_gather | solution.py:121
  9.0 15.1 %copy-start.1 = (bf16[8,16,128,128]{3,2,1,0:T(8,128)(2,1)S(1)}, bf16[8,16,128,128]{3,2,1,0:T(8,128)(2,1)}, u32[]{:S(2)}) copy-start(bf16[8,16,128,128]{3,2,1,0:T(8,128)(2,1)} %param.16) | copy-start | bytes 12582916
  14.3 82.4 %copy-start.14 = (f32[8,8,2,128]{3,2,1,0:T(2,128)}, f32[8,8,2,128]{3,2,1,0:T(2,128)S(1)}, u32[]{:S(2)}) copy-start(f32[8,8,2,128]{3,2,1,0:T(2,128)S(1)} %broadcast_in_dim.22) | copy-start | bytes 196612
  24.1 72.6 %copy-start.6 = (f32[8,16,128]{2,1,0:T(8,128)}, f32[8,16,128]{2,1,0:T(8,128)S(1)}, u32[]{:S(2)}) copy-start(f32[8,16,128]{2,1,0:T(8,128)S(1)} %subtract_multiply_fusion.3) | copy-start | bytes 196612
  32.6 64.1 %copy-start.16 = (f32[8,8,2,128]{3,2,1,0:T(2,128)}, f32[8,8,2,128]{3,2,1,0:T(2,128)S(1)}, u32[]{:S(2)}) copy-start(f32[8,8,2,128]{3,2,1,0:T(2,128)S(1)} %broadcast_in_dim.24) | copy-start | bytes 196612
  41.6 55.1 %copy-start.8 = (f32[8,16,128]{2,1,0:T(8,128)}, f32[8,16,128]{2,1,0:T(8,128)S(1)}, u32[]{:S(2)}) copy-start(f32[8,16,128]{2,1,0:T(8,128)S(1)} %subtract_multiply_fusion.2) | copy-start | bytes 196612
  53.4 43.3 %copy-start.18 = (f32[8,8,2,128]{3,2,1,0:T(2,128)}, f32[8,8,2,128]{3,2,1,0:T(2,128)S(1)}, u32[]{:S(2)}) copy-start(f32[8,8,2,128]{3,2,1,0:T(2,128)S(1)} %broadcast_in_dim.26) | copy-start | bytes 196612
  65.2 31.5 %copy-start.10 = (f32[8,16,128]{2,1,0:T(8,128)}, f32[8,16,128]{2,1,0:T(8,128)S(1)}, u32[]{:S(2)}) copy-start(f32[8,16,128]{2,1,0:T(8,128)S(1)} %subtract_multiply_fusion.1) | copy-start | bytes 196612
  80.9 15.8 %copy-start.20 = (f32[8,8,2,128]{3,2,1,0:T(2,128)}, f32[8,8,2,128]{3,2,1,0:T(2,128)S(1)}, u32[]{:S(2)}) copy-start(f32[8,8,2,128]{3,2,1,0:T(2,128)S(1)} %broadcast_in_dim.28) | copy-start | bytes 196612
  96.6 21.3 %copy-start.12 = (f32[8,16,128]{2,1,0:T(8,128)}, f32[8,16,128]{2,1,0:T(8,128)S(1)}, u32[]{:S(2)}) copy-start(f32[8,16,128]{2,1,0:T(8,128)S(1)} %subtract_multiply_fusion) | copy-start | bytes 196612
  96.7 21.3 %copy-start.5 = (bf16[8,4,2048]{2,1,0:T(4,128)(2,1)S(1)}, bf16[8,4,2048]{2,1,0:T(4,128)(2,1)}, u32[]{:S(2)}) copy-start(bf16[8,4,2048]{2,1,0:T(4,128)(2,1)} %param.20) | copy-start | bytes 393220
  96.8 21.5 %copy-start.25 = (f32[128]{0:T(128)S(1)}, f32[128]{0:T(128)}, u32[]{:S(2)}) copy-start(f32[128]{0:T(128)} %param.27) | copy-start | bytes 1540
  96.8 22.6 %copy-start.22 = (s32[8,4,10]{2,1,0:T(4,128)S(1)}, s32[8,4,10]{2,1,0:T(4,128)}, u32[]{:S(2)}) copy-start(s32[8,4,10]{2,1,0:T(4,128)} %param.24) | copy-start | bytes 3844
  118.2 36.2 %copy-start.4 = (bf16[8,4,2048]{2,1,0:T(4,128)(2,1)S(1)}, bf16[8,4,2048]{2,1,0:T(4,128)(2,1)}, u32[]{:S(2)}) copy-start(bf16[8,4,2048]{2,1,0:T(4,128)(2,1)} %param.23) | copy-start | bytes 393220
  150.7 9.6 %all-to-all-start = ((bf16[8,32,256]{2,1,0:T(8,128)(2,1)}), bf16[8,32,256]{2,1,0:T(8,128)(2,1)S(1)}, u32[]{:S(2)}, u32[]{:S(2)}) async-start(bf16[8,32,256]{2,1,0:T(8,128)(2,1)} %bitcast.64), calls=%async_computation | async-start | bytes 262144 | tf_op jit(solution)/shard_map/all_to_all | solution.py:125
  160.7 11.7 %copy-start.2 = (f32[8,4,2048]{2,1,0:T(4,128)}, f32[8,4,2048]{2,1,0:T(4,128)S(1)}, u32[]{:S(2)}) copy-start(f32[8,4,2048]{2,1,0:T(4,128)S(1)} %reshape.543) | copy-start | bytes 786436
  273.1 43.0 %all-to-all-start.2 = ((bf16[32,8,3,2048]{3,0,2,1:T(8,128)(2,1)}), bf16[32,8,3,2048]{3,0,2,1:T(8,128)(2,1)}, u32[]{:S(2)}, u32[]{:S(2)}) async-start(bf16[32,8,3,2048]{3,0,2,1:T(8,128)(2,1)} %copy.105), calls=%async_computation.2 | async-start | bytes 6291456 | tf_op jit(solution)/shard_map/all_to_all | solution.py:143
  316.1 41.8 %all-to-all-start.5 = ((s32[8,1,1]{2,1,0:T(1,128)}), s32[8,1,1]{2,1,0:T(1,128)S(1)}, u32[]{:S(2)}, u32[]{:S(2)}) async-start(s32[8,1,1]{2,1,0:T(1,128)} %copy.110), calls=%async_computation.5 | async-start | bytes 8192 | tf_op jit(solution)/shard_map/all_to_all | solution.py:113
  357.8 5.8 %copy-start.7 = (f32[8,16,128]{2,1,0:T(8,128)S(1)}, f32[8,16,128]{2,1,0:T(8,128)}, u32[]{:S(2)}) copy-start(f32[8,16,128]{2,1,0:T(8,128)} %copy-done.6) | copy-start | bytes 196612
  357.8 5.8 %copy-start.9 = (f32[8,16,128]{2,1,0:T(8,128)S(1)}, f32[8,16,128]{2,1,0:T(8,128)}, u32[]{:S(2)}) copy-start(f32[8,16,128]{2,1,0:T(8,128)} %copy-done.8) | copy-start | bytes 196612
  357.8 5.8 %copy-start.11 = (f32[8,16,128]{2,1,0:T(8,128)S(1)}, f32[8,16,128]{2,1,0:T(8,128)}, u32[]{:S(2)}) copy-start(f32[8,16,128]{2,1,0:T(8,128)} %copy-done.10) | copy-start | bytes 196612
  357.8 5.9 %copy-start.13 = (f32[8,16,128]{2,1,0:T(8,128)S(1)}, f32[8,16,128]{2,1,0:T(8,128)}, u32[]{:S(2)}) copy-start(f32[8,16,128]{2,1,0:T(8,128)} %copy-done.12) | copy-start | bytes 196612
  357.8 5.9 %copy-start.15 = (f32[8,8,2,128]{3,2,1,0:T(2,128)S(1)}, f32[8,8,2,128]{3,2,1,0:T(2,128)}, u32[]{:S(2)}) copy-start(f32[8,8,2,128]{3,2,1,0:T(2,128)} %copy-done.14) | copy-start | bytes 196612
  357.8 5.9 %copy-start.17 = (f32[8,8,2,128]{3,2,1,0:T(2,128)S(1)}, f32[8,8,2,128]{3,2,1,0:T(2,128)}, u32[]{:S(2)}) copy-start(f32[8,8,2,128]{3,2,1,0:T(2,128)} %copy-done.16) | copy-start | bytes 196612
  357.8 5.9 %copy-start.19 = (f32[8,8,2,128]{3,2,1,0:T(2,128)S(1)}, f32[8,8,2,128]{3,2,1,0:T(2,128)}, u32[]{:S(2)}) copy-start(f32[8,8,2,128]{3,2,1,0:T(2,128)} %copy-done.18) | copy-start | bytes 196612
  357.8 5.9 %copy-start.21 = (f32[8,8,2,128]{3,2,1,0:T(2,128)S(1)}, f32[8,8,2,128]{3,2,1,0:T(2,128)}, u32[]{:S(2)}) copy-start(f32[8,8,2,128]{3,2,1,0:T(2,128)} %copy-done.20) | copy-start | bytes 196612
  357.9 79.9 %all-to-all-start.3 = ((bf16[32,8,3,2048]{3,1,2,0:T(8,128)(2,1)}), bf16[32,8,3,2048]{3,1,2,0:T(8,128)(2,1)}, u32[]{:S(2)}, u32[]{:S(2)}) async-start(bf16[32,8,3,2048]{3,1,2,0:T(8,128)(2,1)} %copy.107), calls=%async_computation.3 | async-start | bytes 6291456 | tf_op jit(solution)/shard_map/all_to_all | solution.py:160
  437.7 54.5 %all-to-all-start.6 = ((bf16[8,1,16,128,128]{4,3,2,1,0:T(8,128)(2,1)}), bf16[8,1,16,128,128]{4,3,2,1,0:T(8,128)(2,1)}, u32[]{:S(2)}, u32[]{:S(2)}) async-start(bf16[8,1,16,128,128]{4,3,2,1,0:T(8,128)(2,1)} %bitcast.132), calls=%async_computation.6 | async-start | bytes 8388608 | tf_op jit(solution)/shard_map/all_to_all | solution.py:110
  447.9 48.8 %copy-start.23 = (f32[8,4,10]{2,1,0:T(4,128)S(1)}, f32[8,4,10]{2,1,0:T(4,128)}, u32[]{:S(2)}) copy-start(f32[8,4,10]{2,1,0:T(4,128)} %param.25) | copy-start | bytes 3844
  447.9 49.0 %copy-start.24 = (s32[320]{0:T(512)S(1)}, s32[320]{0:T(512)}, u32[]{:S(2)}) copy-start(s32[320]{0:T(512)} %fusion.52) | copy-start | bytes 3844
  492.2 42.9 %all-to-all-start.4 = ((bf16[32,8,3,2048]{3,0,2,1:T(8,128)(2,1)}), bf16[32,8,3,2048]{3,0,2,1:T(8,128)(2,1)}, u32[]{:S(2)}, u32[]{:S(2)}) async-start(bf16[32,8,3,2048]{3,0,2,1:T(8,128)(2,1)} %copy.108), calls=%async_computation.4 | async-start | bytes 6291456 | tf_op jit(solution)/shard_map/all_to_all | solution.py:159
  (3 other events, 12.1 us)
Sparse Core Ops, SparseCore 0:
  119.5 28.5 all-gather.1
where the time goes:
time: 577 us; the launch traced here: 571 us
  waiting for transfers between devices  185 us (32%)
  local copies, waits for them, and re-layouts  123 us (21%)
  matrix products  112 us (19%)
  blocking collectives  82.7 us (14%)
  other arithmetic  27.5 us (5%)
  starting transfers between devices  26.7 us (5%)
  between operations  15.4 us (3%)
    all_to_all x1, blocking collectives, shards(): lax.all_to_all(outgoing.reshape(dp_size, ep_size, capacity, model_width),...  82.7 us
    dot_general x4, matrix products, delta_block(): jnp.einsum('bhkv,bhk->bhv', memory_state, queries, precision=lax.Precisio...  56.5 us
    all_to_all x1, waiting for transfers between devices, shards(): lax.all_to_all(result, 'dp', split_axis=0, concat_axis=0, tiled=True)  46.9 us
    dot_general x4, matrix products, delta_block(): jnp.einsum('bhkv,bhk->bhv', memory_state, key_units, precision=lax.Precis...  45.9 us
    all_to_all x1, waiting for transfers between devices, shards(): lax.all_to_all(pack(fresh_states, buffer_index, ep_size), 'ep', split_axi...  44.3 us
    all_to_all x1, waiting for transfers between devices, shards(): lax.all_to_all(lax.all_to_all(outgoing.reshape(dp_size, ep_size, capacity...  36.9 us
    all_gather x1, waiting for transfers between devices, shards(): lax.all_gather(core_flat, 'ep', axis=0, tiled=True)  27.7 us
    all_to_all x1, waiting for transfers between devices, shards(): lax.all_to_all(lax.all_to_all(result, 'dp', split_axis=0, concat_axis=0,...  23.4 us
  transfers between devices with their start and end apart: 7, of which 6 were waited for; matrix products, arithmetic and copies ran while one was open for 16% of the time, Pallas kernels for 0%

commit v1 on v0

--- a/solution.py
+++ b/solution.py
@@ -118,7 +118,9 @@
     token_count = req_count * step_count
     core_flat = core_out.reshape(token_count, core_out.shape[-1])
     columns = jnp.dot(
-        lax.all_gather(core_flat, "ep", axis=0, tiled=True),
+        jnp.concatenate(
+            lax.all_to_all(jnp.stack([core_flat] * lax.axis_size("ep")), "ep", 0, 0), axis=0
+        ),
         out_weight,
         preferred_element_type=jnp.float32,
     ).astype(jnp.bfloat16)

time: 577 us -> 557 us (0.965)
  waiting for transfers between devices: 185 us -> 170 us
  between operations: 15.4 us -> 1.99 us
    all_gather x1 -> x0, waiting for transfers between devices: 27.7 us -> none  [shards(): lax.all_gather(core_flat, 'ep', axis=0, tiled=True)]
    all_to_all x0 -> x1, waiting for transfers between devices: none -> 13.1 us  [shards(): lax.all_to_all(jnp.stack([core_flat] * lax.axis_size('ep')), 'ep', 0, 0)]
where the time goes in v1:
time: 557 us; the launch traced here: 551 us
  waiting for transfers between devices  170 us (31%)
  local copies, waits for them, and re-layouts  124 us (22%)
  matrix products  111 us (20%)
  blocking collectives  84.1 us (15%)
  starting transfers between devices  31.1 us (6%)
  other arithmetic  28.5 us (5%)
    all_to_all x1, blocking collectives, shards(): lax.all_to_all(outgoing.reshape(dp_size, ep_size, capacity, model_width),...  84.1 us
    dot_general x4, matrix products, delta_block(): jnp.einsum('bhkv,bhk->bhv', memory_state, queries, precision=lax.Precisio...  56.5 us
    all_to_all x1, waiting for transfers between devices, shards(): lax.all_to_all(result, 'dp', split_axis=0, concat_axis=0, tiled=True)  46.9 us
    dot_general x4, matrix products, delta_block(): jnp.einsum('bhkv,bhk->bhv', memory_state, key_units, precision=lax.Precis...  45.9 us
    all_to_all x1, waiting for transfers between devices, shards(): lax.all_to_all(pack(fresh_states, buffer_index, ep_size), 'ep', split_axi...  44.3 us
    all_to_all x1, waiting for transfers between devices, shards(): lax.all_to_all(lax.all_to_all(outgoing.reshape(dp_size, ep_size, capacity...  36.9 us
    all_to_all x1, waiting for transfers between devices, shards(): lax.all_to_all(lax.all_to_all(result, 'dp', split_axis=0, concat_axis=0,...  23.4 us
    reshape x2, local copies, waits for them, and re-layouts, shards(): expert_apply(arrived.reshape(-1, model_width), gate_up[0], down_weight[0])  16.3 us
  transfers between devices with their start and end apart: 7, of which 6 were waited for; matrix products, arithmetic and copies ran while one was open for 16% of the time, Pallas kernels for 0%

profile of v1, /device:TPU:24, one launch (start us, length us, event | category | flops | bytes accessed | tf_op | source)
XLA Modules:
  0.0 550.8 jit_solution(10348469416959453216)
XLA Ops:
  7.7 9.7 %fusion = f32[8,16,1,128]{3,2,1,0:T(1,128)S(1)} fusion(f32[8,16,128,1]{2,3,1,0:T(1,128)S(1)} %bitcast.154, bf16[8,16,128,128]{3,2,1,0:T(8,128)(2,1)} %param.16, f32[8,16]{1,0:T(8,128)S(1)} %get-tuple-element.37), kind=kOutput, calls=%fused_computation.10 | convolution fusion | flops 29360128 | bytes 4325888 | tf_op jit(solution)/shard_map/bhkv,bhk->bhv/dot_general | solution.py:38
  17.6 8.3 %fusion.2 = f32[8,16,1,128]{3,2,1,0:T(1,128)S(1)} fusion(f32[8,16,128,1]{2,3,1,0:T(1,128)S(1)} %bitcast.198, bf16[8,16,128,128]{3,2,1,0:T(8,128)(2,1)S(1)} %copy-done.1, f32[8,16,128]{2,1,0:T(8,128)S(1)} %subtract_multiply_fusion.3, f32[8,16,128]{2,1,0:T(8,128)S(1)} %bitcast.155, f32[8,16]{1,0:T(8,128)S(1)} %get-tuple-element.37), kind=kOutput, calls=%fused_computation.12 | convolution fusion | flops 33554432 | bytes 4456960 | tf_op jit(solution)/shard_map/bhkv,bhk->bhv/dot_general | solution.py:43
  26.0 9.0 %fusion.3 = f32[8,16,1,128]{3,2,1,0:T(1,128)S(1)} fusion(f32[8,16,128,1]{2,3,1,0:T(1,128)S(1)} %bitcast.163, bf16[8,16,128,128]{3,2,1,0:T(8,128)(2,1)S(1)} %copy-done.1, f32[8,16]{1,0:T(8,128)S(1)} %get-tuple-element.36, f32[8,16,128]{2,1,0:T(8,128)S(1)} %subtract_multiply_fusion.3, f32[8,16,128]{2,1,0:T(8,128)S(1)} %bitcast.156, ...), kind=kOutput, calls=%fused_computation.13 | convolution fusion | flops 35651584 | bytes 4457472 | tf_op jit(solution)/shard_map/bhkv,bhk->bhv/dot_general | solution.py:38
  35.1 11.6 %fusion.11 = f32[8,16,1,128]{3,2,1,0:T(1,128)S(1)} fusion(f32[8,16,128,1]{2,3,1,0:T(1,128)S(1)} %bitcast.199, bf16[8,16,128,128]{3,2,1,0:T(8,128)(2,1)S(1)} %copy-done.1, f32[8,16,128]{2,1,0:T(8,128)S(1)} %subtract_multiply_fusion.2, f32[8,16,128]{2,1,0:T(8,128)S(1)} %bitcast.164, f32[8,16]{1,0:T(8,128)S(1)} %get-tuple-element.36, ...), kind=kOutput, calls=%fused_computation.20 | convolution fusion | flops 39845888 | bytes 4588544 | tf_op jit(solution)/shard_map/bhkv,bhk->bhv/dot_general | solution.py:43
  46.9 11.7 %fusion.7 = f32[8,16,1,128]{3,2,1,0:T(1,128)S(1)} fusion(f32[8,16,128,1]{2,3,1,0:T(1,128)S(1)} %bitcast.170, bf16[8,16,128,128]{3,2,1,0:T(8,128)(2,1)S(1)} %copy-done.1, f32[8,16]{1,0:T(8,128)S(1)} %get-tuple-element.35, f32[8,16,128]{2,1,0:T(8,128)S(1)} %subtract_multiply_fusion.2, f32[8,16,128]{2,1,0:T(8,128)S(1)} %bitcast.165, ...), kind=kOutput, calls=%fused_computation.16 | convolution fusion | flops 41943040 | bytes 4589056 | tf_op jit(solution)/shard_map/bhkv,bhk->bhv/dot_general | solution.py:38
  58.7 15.5 %fusion.43 = f32[8,16,1,128]{3,2,1,0:T(1,128)S(1)} fusion(f32[8,16,128,1]{2,3,1,0:T(1,128)S(1)} %bitcast.200, bf16[8,16,128,128]{3,2,1,0:T(8,128)(2,1)S(1)} %copy-done.1, f32[8,16,128]{2,1,0:T(8,128)S(1)} %subtract_multiply_fusion.1, f32[8,16,128]{2,1,0:T(8,128)S(1)} %bitcast.171, f32[8,16]{1,0:T(8,128)S(1)} %get-tuple-element.35, ...), kind=kOutput, calls=%fused_computation.56 | convolution fusion | flops 46137344 | bytes 4720128 | tf_op jit(solution)/shard_map/bhkv,bhk->bhv/dot_general | solution.py:43
  74.3 15.6 %fusion.5 = f32[8,16,1,128]{3,2,1,0:T(1,128)S(1)} fusion(f32[8,16,128,1]{2,3,1,0:T(1,128)S(1)} %bitcast.175, f32[8,16]{1,0:T(8,128)S(1)} %get-tuple-element.34, bf16[8,16,128,128]{3,2,1,0:T(8,128)(2,1)S(1)} %copy-done.1, f32[8,16,128]{2,1,0:T(8,128)S(1)} %subtract_multiply_fusion.1, f32[8,16,128]{2,1,0:T(8,128)S(1)} %bitcast.172, ...), kind=kOutput, calls=%fused_computation.14 | convolution fusion | flops 48234496 | bytes 4720640 | tf_op jit(solution)/shard_map/bhkv,bhk->bhv/dot_general | solution.py:38
  90.2 21.1 %fusion.10 = f32[8,16,1,128]{3,2,1,0:T(1,128)S(1)} fusion(f32[8,16,128,1]{2,3,1,0:T(1,128)S(1)} %bitcast.201, f32[8,16,128]{2,1,0:T(8,128)S(1)} %subtract_multiply_fusion, f32[8,16,128]{2,1,0:T(8,128)S(1)} %bitcast.176, f32[8,16]{1,0:T(8,128)S(1)} %get-tuple-element.34, bf16[8,16,128,128]{3,2,1,0:T(8,128)(2,1)S(1)} %copy-done.1, ...), kind=kOutput, calls=%fused_computation.19 | convolution fusion | flops 52428800 | bytes 4851712 | tf_op jit(solution)/shard_map/bhkv,bhk->bhv/dot_general | solution.py:43
  120.5 13.1 %all-to-all-done = bf16[8,32,2048]{2,1,0:T(8,128)(2,1)S(1)} async-done(((bf16[8,32,2048]{2,1,0:T(8,128)(2,1)}), bf16[8,32,2048]{2,1,0:T(8,128)(2,1)S(1)}, u32[]{:S(2)}, u32[]{:S(2)}) %all-to-all-start) | async-done | bytes 1048608 | tf_op jit(solution)/shard_map/all_to_all | solution.py:122
  140.2 5.3 all-to-all-done.1
  152.1 5.4 scatter_custom_fusion
  157.5 9.1 %reshape.506 = bf16[32,8,3,2048]{3,2,1,0:T(4,128)(2,1)} reshape(bf16[768,2048]{1,0:T(8,128)(2,1)} %scatter_custom_fusion) | data formatting | bytes 6291456 | tf_op jit(solution)/shard_map/reshape | solution.py:147
  166.6 5.5 copy.104
  172.1 84.1 %all_to_all.55 = bf16[32,8,3,2048]{3,1,2,0:T(8,128)(2,1)S(1)} all-to-all(bf16[32,8,3,2048]{3,1,2,0:T(8,128)(2,1)S(1)} %copy.104), channel_id=1, replica_groups=mesh['dp'=32,'ep'=8] {'dp'}, dimensions={0} | all-to-all | bytes 6291456 | tf_op jit(solution)/shard_map/all_to_all | solution.py:146
  259.6 4.6 all-to-all-start.3
  265.7 36.9 %all-to-all-done.3 = bf16[32,8,3,2048]{3,0,2,1:T(8,128)(2,1)} async-done(((bf16[32,8,3,2048]{3,0,2,1:T(8,128)(2,1)}), bf16[32,8,3,2048]{3,0,2,1:T(8,128)(2,1)}, u32[]{:S(2)}, u32[]{:S(2)}) %all-to-all-start.3) | async-done | bytes 3145760 | tf_op jit(solution)/shard_map/all_to_all | solution.py:145
  306.1 6.6 %copy.106 = bf16[32,8,3,2048]{3,2,1,0:T(4,128)(2,1)} copy(bf16[32,8,3,2048]{3,0,2,1:T(8,128)(2,1)} %all-to-all-done.3) | data formatting | bytes 6291456 | tf_op jit(solution)/shard_map/all_to_all | solution.py:145
  312.7 8.8 %reshape.507 = bf16[768,2048]{1,0:T(8,128)(2,1)} reshape(bf16[32,8,3,2048]{3,2,1,0:T(4,128)(2,1)} %copy.106) | data formatting | bytes 6291456 | tf_op jit(solution)/shard_map/reshape | solution.py:158
  328.0 9.1 %reshape.508 = bf16[32,8,3,2048]{3,2,1,0:T(4,128)(2,1)} reshape(bf16[768,2048]{1,0:T(8,128)(2,1)} %convolution_convert_fusion) | data formatting | bytes 6291456 | tf_op jit(solution)/shard_map/reshape | solution.py:158
  337.1 7.2 %copy.107 = bf16[32,8,3,2048]{3,1,2,0:T(8,128)(2,1)} copy(bf16[32,8,3,2048]{3,2,1,0:T(4,128)(2,1)} %reshape.508) | data formatting | bytes 6291456 | tf_op jit(solution)/shard_map/reshape | solution.py:158
  344.4 5.8 %all-to-all-start.4 = ((bf16[32,8,3,2048]{3,1,2,0:T(8,128)(2,1)}), bf16[32,8,3,2048]{3,1,2,0:T(8,128)(2,1)}, u32[]{:S(2)}, u32[]{:S(2)}) async-start(bf16[32,8,3,2048]{3,1,2,0:T(8,128)(2,1)} %copy.107), calls=%async_computation.4 | async-start | bytes 6291456 | tf_op jit(solution)/shard_map/all_to_all | solution.py:162
  350.3 13.3 %fusion.9 = bf16[8,16,128,128]{3,2,1,0:T(8,128)(2,1)} fusion(f32[8,16,128]{2,1,0:T(8,128)S(1)} %copy-done.14, f32[8,16,128]{2,1,0:T(8,128)S(1)} %bitcast.177, f32[8,16]{1,0:T(8,128)S(1)} %get-tuple-element.34, f32[8,16,128]{2,1,0:T(8,128)S(1)} %copy-done.12, f32[8,16,128]{2,1,0:T(8,128)S(1)} %bitcast.174, f32[8,16]{1,0:T(8,128)S(1)} %get-tuple-element.35, ...), kind=kLoop, calls=%fused_computation.18 | loop fusion | flops 29360128 | bytes 8914944 | tf_op jit(solution)/shard_map/convert_element_type | solution.py:52
  366.6 10.9 %scatter_fusion = bf16[8,16,128,128]{3,2,1,0:T(8,128)(2,1)} fusion(bf16[8,16,128,128]{3,2,1,0:T(8,128)(2,1)} %broadcast.333.clone, s32[8]{0:T(128)S(1)} %compare_select_fusion.2, bf16[8,16,128,128]{3,2,1,0:T(8,128)(2,1)} %fusion.9), kind=kCustom, calls=%fused_computation.3 | custom fusion | bytes 12582944 | tf_op jit(solution)/shard_map/scatter | solution.py:68
  377.4 46.9 %all-to-all-done.4 = bf16[32,8,3,2048]{3,1,2,0:T(8,128)(2,1)} async-done(((bf16[32,8,3,2048]{3,1,2,0:T(8,128)(2,1)}), bf16[32,8,3,2048]{3,1,2,0:T(8,128)(2,1)}, u32[]{:S(2)}, u32[]{:S(2)}) %all-to-all-start.4) | async-done | bytes 3145760 | tf_op jit(solution)/shard_map/all_to_all | solution.py:162
  424.3 4.8 all-to-all-start.7
  429.1 5.3 copy.108
  434.4 44.3 %all-to-all-done.7 = bf16[8,1,16,128,128]{4,3,2,1,0:T(8,128)(2,1)} async-done(((bf16[8,1,16,128,128]{4,3,2,1,0:T(8,128)(2,1)}), bf16[8,1,16,128,128]{4,3,2,1,0:T(8,128)(2,1)}, u32[]{:S(2)}, u32[]{:S(2)}) %all-to-all-start.7) | async-done | bytes 4194336 | tf_op jit(solution)/shard_map/all_to_all | solution.py:110
  487.4 10.9 %scatter_fusion.1 = bf16[8,16,128,128]{3,2,1,0:T(8,128)(2,1)} fusion(bf16[8,16,128,128]{3,2,1,0:T(8,128)(2,1)} %broadcast.333, s32[8]{0:T(128)S(1)} %fusion.54, bf16[8,16,128,128]{3,2,1,0:T(8,128)(2,1)} %bitcast.78), kind=kCustom, calls=%fused_computation.4 | custom fusion | bytes 12582944 | tf_op jit(solution)/shard_map/scatter | solution.py:117
  498.2 23.4 %all-to-all-done.5 = bf16[32,8,3,2048]{3,0,2,1:T(8,128)(2,1)} async-done(((bf16[32,8,3,2048]{3,0,2,1:T(8,128)(2,1)}), bf16[32,8,3,2048]{3,0,2,1:T(8,128)(2,1)}, u32[]{:S(2)}, u32[]{:S(2)}) %all-to-all-start.5) | async-done | bytes 3145760 | tf_op jit(solution)/shard_map/all_to_all | solution.py:161
  521.7 6.5 %copy.109 = bf16[32,8,3,2048]{3,2,1,0:T(4,128)(2,1)} copy(bf16[32,8,3,2048]{3,0,2,1:T(8,128)(2,1)} %all-to-all-done.5) | data formatting | bytes 6291456 | tf_op jit(solution)/shard_map/all_to_all | solution.py:161
  528.2 8.8 %reshape.509 = bf16[768,2048]{1,0:T(8,128)(2,1)} reshape(bf16[32,8,3,2048]{3,2,1,0:T(4,128)(2,1)} %copy.109) | data formatting | bytes 6291456 | tf_op jit(solution)/shard_map/reshape | solution.py:168
  537.0 6.8 %gather_fusion = bf16[320,2048]{1,0:T(8,128)(2,1)S(1)} fusion(bf16[768,2048]{1,0:T(8,128)(2,1)} %reshape.509, s32[1024]{0:T(1024)} %pad_clamp_fusion), kind=kCustom, calls=%fused_computation | custom fusion | bytes 2622720 | tf_op jit(solution)/shard_map/gather | solution.py:168
  (171 shorter events, 63.1 us)
Async XLA Ops:
  0.6 320.9 %copy-start = (bf16[1,2048,512]{2,1,0:T(8,128)(2,1)S(1)}, bf16[1,2048,512]{2,1,0:T(8,128)(2,1)}, u32[]{:S(2)}) copy-start(bf16[1,2048,512]{2,1,0:T(8,128)(2,1)} %param.29) | copy-start | bytes 6291460
  2.4 15.1 %copy-start.1 = (bf16[8,16,128,128]{3,2,1,0:T(8,128)(2,1)S(1)}, bf16[8,16,128,128]{3,2,1,0:T(8,128)(2,1)}, u32[]{:S(2)}) copy-start(bf16[8,16,128,128]{3,2,1,0:T(8,128)(2,1)} %param.16) | copy-start | bytes 12582916
  7.7 82.4 %copy-start.15 = (f32[8,8,2,128]{3,2,1,0:T(2,128)}, f32[8,8,2,128]{3,2,1,0:T(2,128)S(1)}, u32[]{:S(2)}) copy-start(f32[8,8,2,128]{3,2,1,0:T(2,128)S(1)} %broadcast_in_dim.22) | copy-start | bytes 196612
  17.5 72.6 %copy-start.7 = (f32[8,16,128]{2,1,0:T(8,128)}, f32[8,16,128]{2,1,0:T(8,128)S(1)}, u32[]{:S(2)}) copy-start(f32[8,16,128]{2,1,0:T(8,128)S(1)} %subtract_multiply_fusion.3) | copy-start | bytes 196612
  26.0 64.1 %copy-start.17 = (f32[8,8,2,128]{3,2,1,0:T(2,128)}, f32[8,8,2,128]{3,2,1,0:T(2,128)S(1)}, u32[]{:S(2)}) copy-start(f32[8,8,2,128]{3,2,1,0:T(2,128)S(1)} %broadcast_in_dim.24) | copy-start | bytes 196612
  35.1 55.1 %copy-start.9 = (f32[8,16,128]{2,1,0:T(8,128)}, f32[8,16,128]{2,1,0:T(8,128)S(1)}, u32[]{:S(2)}) copy-start(f32[8,16,128]{2,1,0:T(8,128)S(1)} %subtract_multiply_fusion.2) | copy-start | bytes 196612
  46.9 43.3 %copy-start.19 = (f32[8,8,2,128]{3,2,1,0:T(2,128)}, f32[8,8,2,128]{3,2,1,0:T(2,128)S(1)}, u32[]{:S(2)}) copy-start(f32[8,8,2,128]{3,2,1,0:T(2,128)S(1)} %broadcast_in_dim.26) | copy-start | bytes 196612
  58.6 31.5 %copy-start.11 = (f32[8,16,128]{2,1,0:T(8,128)}, f32[8,16,128]{2,1,0:T(8,128)S(1)}, u32[]{:S(2)}) copy-start(f32[8,16,128]{2,1,0:T(8,128)S(1)} %subtract_multiply_fusion.1) | copy-start | bytes 196612
  74.3 15.8 %copy-start.21 = (f32[8,8,2,128]{3,2,1,0:T(2,128)}, f32[8,8,2,128]{3,2,1,0:T(2,128)S(1)}, u32[]{:S(2)}) copy-start(f32[8,8,2,128]{3,2,1,0:T(2,128)S(1)} %broadcast_in_dim.28) | copy-start | bytes 196612
  90.1 21.3 %copy-start.13 = (f32[8,16,128]{2,1,0:T(8,128)}, f32[8,16,128]{2,1,0:T(8,128)S(1)}, u32[]{:S(2)}) copy-start(f32[8,16,128]{2,1,0:T(8,128)S(1)} %subtract_multiply_fusion) | copy-start | bytes 196612
  90.2 21.3 %copy-start.6 = (bf16[8,4,2048]{2,1,0:T(4,128)(2,1)S(1)}, bf16[8,4,2048]{2,1,0:T(4,128)(2,1)}, u32[]{:S(2)}) copy-start(bf16[8,4,2048]{2,1,0:T(4,128)(2,1)} %param.20) | copy-start | bytes 393220
  90.2 21.5 %copy-start.26 = (f32[128]{0:T(128)S(1)}, f32[128]{0:T(128)}, u32[]{:S(2)}) copy-start(f32[128]{0:T(128)} %param.27) | copy-start | bytes 1540
  111.3 6.3 %copy-start.23 = (s32[8,4,10]{2,1,0:T(4,128)S(1)}, s32[8,4,10]{2,1,0:T(4,128)}, u32[]{:S(2)}) copy-start(s32[8,4,10]{2,1,0:T(4,128)} %param.24) | copy-start | bytes 3844
  113.2 26.4 %copy-start.5 = (bf16[8,4,2048]{2,1,0:T(4,128)(2,1)S(1)}, bf16[8,4,2048]{2,1,0:T(4,128)(2,1)}, u32[]{:S(2)}) copy-start(bf16[8,4,2048]{2,1,0:T(4,128)(2,1)} %param.23) | copy-start | bytes 393220
  113.2 20.4 %all-to-all-start = ((bf16[8,32,2048]{2,1,0:T(8,128)(2,1)}), bf16[8,32,2048]{2,1,0:T(8,128)(2,1)S(1)}, u32[]{:S(2)}, u32[]{:S(2)}) async-start(bf16[8,32,2048]{2,1,0:T(8,128)(2,1)} %stack.5), calls=%async_computation | async-start | bytes 2097152 | tf_op jit(solution)/shard_map/all_to_all | solution.py:122
  135.9 9.6 %all-to-all-start.1 = ((bf16[8,32,256]{2,1,0:T(8,128)(2,1)}), bf16[8,32,256]{2,1,0:T(8,128)(2,1)S(1)}, u32[]{:S(2)}, u32[]{:S(2)}) async-start(bf16[8,32,256]{2,1,0:T(8,128)(2,1)} %bitcast.65), calls=%async_computation.1 | async-start | bytes 262144 | tf_op jit(solution)/shard_map/all_to_all | solution.py:127
  145.9 11.7 %copy-start.2 = (f32[8,4,2048]{2,1,0:T(4,128)}, f32[8,4,2048]{2,1,0:T(4,128)S(1)}, u32[]{:S(2)}) copy-start(f32[8,4,2048]{2,1,0:T(4,128)S(1)} %reshape.545) | copy-start | bytes 786436
  259.6 43.0 %all-to-all-start.3 = ((bf16[32,8,3,2048]{3,0,2,1:T(8,128)(2,1)}), bf16[32,8,3,2048]{3,0,2,1:T(8,128)(2,1)}, u32[]{:S(2)}, u32[]{:S(2)}) async-start(bf16[32,8,3,2048]{3,0,2,1:T(8,128)(2,1)} %copy.105), calls=%async_computation.3 | async-start | bytes 6291456 | tf_op jit(solution)/shard_map/all_to_all | solution.py:145
  302.6 41.8 %all-to-all-start.6 = ((s32[8,1,1]{2,1,0:T(1,128)}), s32[8,1,1]{2,1,0:T(1,128)S(1)}, u32[]{:S(2)}, u32[]{:S(2)}) async-start(s32[8,1,1]{2,1,0:T(1,128)} %copy.110), calls=%async_computation.6 | async-start | bytes 8192 | tf_op jit(solution)/shard_map/all_to_all | solution.py:113
  344.3 5.8 %copy-start.8 = (f32[8,16,128]{2,1,0:T(8,128)S(1)}, f32[8,16,128]{2,1,0:T(8,128)}, u32[]{:S(2)}) copy-start(f32[8,16,128]{2,1,0:T(8,128)} %copy-done.7) | copy-start | bytes 196612
  344.3 5.8 %copy-start.10 = (f32[8,16,128]{2,1,0:T(8,128)S(1)}, f32[8,16,128]{2,1,0:T(8,128)}, u32[]{:S(2)}) copy-start(f32[8,16,128]{2,1,0:T(8,128)} %copy-done.9) | copy-start | bytes 196612
  344.3 5.8 %copy-start.12 = (f32[8,16,128]{2,1,0:T(8,128)S(1)}, f32[8,16,128]{2,1,0:T(8,128)}, u32[]{:S(2)}) copy-start(f32[8,16,128]{2,1,0:T(8,128)} %copy-done.11) | copy-start | bytes 196612
  344.4 5.9 %copy-start.14 = (f32[8,16,128]{2,1,0:T(8,128)S(1)}, f32[8,16,128]{2,1,0:T(8,128)}, u32[]{:S(2)}) copy-start(f32[8,16,128]{2,1,0:T(8,128)} %copy-done.13) | copy-start | bytes 196612
  344.4 5.9 %copy-start.16 = (f32[8,8,2,128]{3,2,1,0:T(2,128)S(1)}, f32[8,8,2,128]{3,2,1,0:T(2,128)}, u32[]{:S(2)}) copy-start(f32[8,8,2,128]{3,2,1,0:T(2,128)} %copy-done.15) | copy-start | bytes 196612
  344.4 5.9 %copy-start.18 = (f32[8,8,2,128]{3,2,1,0:T(2,128)S(1)}, f32[8,8,2,128]{3,2,1,0:T(2,128)}, u32[]{:S(2)}) copy-start(f32[8,8,2,128]{3,2,1,0:T(2,128)} %copy-done.17) | copy-start | bytes 196612
  344.4 5.9 %copy-start.20 = (f32[8,8,2,128]{3,2,1,0:T(2,128)S(1)}, f32[8,8,2,128]{3,2,1,0:T(2,128)}, u32[]{:S(2)}) copy-start(f32[8,8,2,128]{3,2,1,0:T(2,128)} %copy-done.19) | copy-start | bytes 196612
  344.4 5.9 %copy-start.22 = (f32[8,8,2,128]{3,2,1,0:T(2,128)S(1)}, f32[8,8,2,128]{3,2,1,0:T(2,128)}, u32[]{:S(2)}) copy-start(f32[8,8,2,128]{3,2,1,0:T(2,128)} %copy-done.21) | copy-start | bytes 196612
  344.4 79.9 %all-to-all-start.4 = ((bf16[32,8,3,2048]{3,1,2,0:T(8,128)(2,1)}), bf16[32,8,3,2048]{3,1,2,0:T(8,128)(2,1)}, u32[]{:S(2)}, u32[]{:S(2)}) async-start(bf16[32,8,3,2048]{3,1,2,0:T(8,128)(2,1)} %copy.107), calls=%async_computation.4 | async-start | bytes 6291456 | tf_op jit(solution)/shard_map/all_to_all | solution.py:162
  424.3 54.5 %all-to-all-start.7 = ((bf16[8,1,16,128,128]{4,3,2,1,0:T(8,128)(2,1)}), bf16[8,1,16,128,128]{4,3,2,1,0:T(8,128)(2,1)}, u32[]{:S(2)}, u32[]{:S(2)}) async-start(bf16[8,1,16,128,128]{4,3,2,1,0:T(8,128)(2,1)} %bitcast.133), calls=%async_computation.7 | async-start | bytes 8388608 | tf_op jit(solution)/shard_map/all_to_all | solution.py:110
  434.4 48.8 %copy-start.24 = (f32[8,4,10]{2,1,0:T(4,128)S(1)}, f32[8,4,10]{2,1,0:T(4,128)}, u32[]{:S(2)}) copy-start(f32[8,4,10]{2,1,0:T(4,128)} %param.25) | copy-start | bytes 3844
  434.4 49.0 %copy-start.25 = (s32[320]{0:T(512)S(1)}, s32[320]{0:T(512)}, u32[]{:S(2)}) copy-start(s32[320]{0:T(512)} %fusion.52) | copy-start | bytes 3844
  478.8 42.9 %all-to-all-start.5 = ((bf16[32,8,3,2048]{3,0,2,1:T(8,128)(2,1)}), bf16[32,8,3,2048]{3,0,2,1:T(8,128)(2,1)}, u32[]{:S(2)}, u32[]{:S(2)}) async-start(bf16[32,8,3,2048]{3,0,2,1:T(8,128)(2,1)} %copy.108), calls=%async_computation.5 | async-start | bytes 6291456 | tf_op jit(solution)/shard_map/all_to_all | solution.py:161
  (4 other events, 12.9 us)
